TPU v7x, 512 devices: a whole 4x4x16 slice. The times are simulated.
512 devices in a mesh: mesh: 64 (over y, z), obs: 8 (over x, core).
Axes of the slice: x: 4, y: 4, z: 16, core: 2. Of those that a mesh axis runs over, the one named last changes fastest.
Arguments:
- probes: bfloat16 [64, 512, 2048], P(None, 'mesh', 'obs'), may hold values from -6 to 6
- velocity: float32 [512, 2048], P('mesh', 'obs'), may hold values from 0.5 to 2
- viscosity: float32 [512, 2048], P('mesh', 'obs'), may hold values from 0.1 to 3
- friction: float32 [512, 2048], P('mesh', 'obs'), may hold values from 0.5 to 4
- obs_block: int32 [64, 512], P('mesh', 'obs'), may hold values from 0 to 127
- obs_weight: float32 [64, 512, 128], P('mesh', 'obs'), may hold values from -0.5 to 0.5
- obs_prec: float32 [64, 512], P('mesh', 'obs'), may hold values from 0.05 to 0.5
- rank: int32 [1], replicated, may hold values from 1 to 64
Outputs:
- basis: float32 [64, 512, 2048], P(None, 'mesh', 'obs')
- factor: float32 [64, 64], replicated
All inputs are finite; a program needn't handle non-finite values.
Results may differ from a plain program's by a relative error of at most 0.0027.
Values may be sent and summed in bfloat16 or wider, within the bound.
A program may use at most 64 MiB of HBM per device.

v0:
```python
import jax
import jax.numpy as jnp
from jax import lax
from jax.sharding import PartitionSpec as P

BLOCK = 128
PRIOR = 1.0


def extended(block, sides, width):
    for axis, dim in sides:
        count = lax.axis_size(axis)
        forward = [(i, i + 1) for i in range(count - 1)]
        backward = [(target, source) for source, target in forward]
        low = lax.ppermute(
            lax.slice_in_dim(block, block.shape[dim] - width, None, axis=dim), axis, forward
        )
        high = lax.ppermute(lax.slice_in_dim(block, 0, width, axis=dim), axis, backward)
        block = jnp.concatenate([low, block, high], axis=dim)
    return block


def apply_padded(padded, visc_pad, friction):
    height = padded.shape[1] - 2
    width = padded.shape[2] - 2
    centre = padded[:, 1:-1, 1:-1]
    visc_mid = visc_pad[1:-1, 1:-1]
    result = friction * centre
    for shift_row, shift_col in ((2, 1), (0, 1), (1, 2), (1, 0)):
        neighbor = padded[:, shift_row : shift_row + height, shift_col : shift_col + width]
        face_coef = 0.5 * (
            visc_mid + visc_pad[shift_row : shift_row + height, shift_col : shift_col + width]
        )
        result = result + face_coef * (centre - neighbor)
    return result


def per_device(probes, velocity, viscosity, friction, obs_block, obs_weight, obs_prec, rank):
    probe_count = probes.shape[0]
    rows_here, cols_here = velocity.shape
    obs_devices = lax.axis_size("obs")
    slab_columns = cols_here * obs_devices // BLOCK
    owned_blocks = cols_here // BLOCK
    cell_total = rows_here * cols_here * lax.axis_size("mesh") * obs_devices
    omega = probes.astype(jnp.float32)
    stacked = jnp.concatenate([velocity[None] * omega, viscosity[None]], axis=0)
    padded = extended(stacked, (("mesh", 1), ("obs", 2)), 1)
    visc_pad = padded[-1]
    tangent = apply_padded(padded[:-1], visc_pad, friction).astype(jnp.bfloat16)
    row_ids = obs_block[0] // slab_columns
    col_ids = obs_block[0] % slab_columns
    weights = obs_weight[0]
    precision = obs_prec[0]
    segment = lax.all_gather(tangent, "obs", axis=2, tiled=True)
    seg_blocks = segment.shape[2] // BLOCK
    local_col = col_ids
    inside = (local_col >= 0) & (local_col < seg_blocks)
    block_index = row_ids * seg_blocks + jnp.clip(local_col, 0, seg_blocks - 1)
    blocks = segment.reshape(probe_count, rows_here * seg_blocks, BLOCK)
    picked = jnp.take(blocks, block_index, axis=1).astype(jnp.float32)
    value = precision * jnp.sum(picked * weights, axis=-1)
    misfit = jnp.where(inside, value, 0.0)
    amount = lax.axis_size("obs") * owned_blocks
    local_col = col_ids
    inside = (local_col >= 0) & (local_col < amount)
    block_index = jnp.clip(local_col, 0, amount - 1) * rows_here + row_ids
    contrib = jnp.where(inside[None, :, None], misfit[:, :, None] * weights[None], 0.0)
    partial_value = (
        jnp.zeros((probe_count, amount * rows_here, BLOCK), jnp.float32)
        .at[:, block_index]
        .add(contrib)
    )
    received = lax.psum_scatter(
        partial_value.reshape(probe_count, amount, rows_here, BLOCK).transpose(1, 0, 2, 3),
        "obs",
        scatter_dimension=0,
        tiled=True,
    )
    source = received.transpose(1, 2, 0, 3).reshape(probe_count, rows_here, cols_here)
    padded_source = extended(source, (("mesh", 1), ("obs", 2)), 1)
    gradient = velocity * apply_padded(padded_source, visc_pad, friction)
    sketch = (gradient + PRIOR * omega).reshape(probe_count, rows_here * cols_here)
    local_gram = (
        jnp.dot(
            sketch, sketch.T, precision=lax.Precision.HIGHEST, preferred_element_type=jnp.float32
        )
        / cell_total
    )
    factor = jnp.linalg.cholesky(lax.psum(local_gram, ("mesh", "obs")))
    solved = lax.linalg.triangular_solve(factor, sketch, left_side=True, lower=True)
    retained = (jnp.arange(probe_count, dtype=jnp.int32) < rank[0])[:, None]
    basis = jnp.where(retained, solved, 0.0).reshape(probe_count, rows_here, cols_here)
    return (basis, factor)


def solution(mesh):
    in_specs = (
        P(None, "mesh", "obs"),
        P("mesh", "obs"),
        P("mesh", "obs"),
        P("mesh", "obs"),
        P("mesh", "obs"),
        P("mesh", "obs", None),
        P("mesh", "obs"),
        P(),
    )
    out_specs = (P(None, "mesh", "obs"), P())
    return jax.shard_map(
        per_device, mesh=mesh, in_specs=in_specs, out_specs=out_specs, check_vma=False
    )
```

profile of v0, /device:TPU:1, one launch (start us, length us, event | category | flops | bytes accessed | tf_op | source)
XLA Modules:
  0.0 289.0 jit_solution(15032128486639405339)
XLA Ops:
  7.2 0.0 all-gather.2.cloned.1.call-start
  7.2 1.0 convert_multiply_fusion
  8.2 0.9 pad_maximum_fusion.23
  9.1 4.4 %collective-permute-start = (f32[65,1,256]{2,0,1:T(8,128)S(1)}, f32[65,1,256]{2,0,1:T(8,128)S(1)}, u32[]{:S(2)}, u32[]{:S(2)}) collective-permute-start(f32[65,1,256]{2,0,1:T(8,128)S(1)} %copy.38), channel_id=1, source_target_pairs={{0,8},{8,16},{16,24},{24,32},{32,40},{40,48},{48,56},{56,64},{64,7... | collective-permute-start | bytes 199688 | tf_op jit(solution)/shard_map/ppermute | solution.py:15
  13.5 1.3 collective-permute-start.1
  14.8 0.1 collective-permute-done
  14.9 0.1 copy.40
  14.9 3.8 %collective-permute-done.1 = f32[65,1,256]{2,0,1:T(8,128)S(1)} collective-permute-done((f32[65,1,256]{2,0,1:T(8,128)S(1)}, f32[65,1,256]{2,0,1:T(8,128)S(1)}, u32[]{:S(2)}, u32[]{:S(2)}) %collective-permute-start.1) | collective-permute-done | bytes 66592 | tf_op jit(solution)/shard_map/ppermute | solution.py:18
  18.8 0.1 copy.41
  18.8 0.9 pad_maximum_fusion
  19.7 0.0 copy-start.2
  19.7 0.2 fusion.39
  19.9 0.0 copy-start.4
  20.0 0.3 copy.42
  20.2 4.9 %collective-permute-start.2 = (f32[65,10,1]{0,1,2:T(8,128)S(1)}, f32[65,10,1]{0,1,2:T(8,128)S(1)}, u32[]{:S(2)}, u32[]{:S(2)}) collective-permute-start(f32[65,10,1]{0,1,2:T(8,128)S(1)} %copy.42), channel_id=1, source_target_pairs={{0,1},{1,2},{2,3},{3,4},{4,5},{5,6},{6,7},{8,9},{9,10},{10,11},{11... | collective-permute-start | bytes 7808 | tf_op jit(solution)/shard_map/ppermute | solution.py:15
  25.2 0.3 copy.43
  25.4 3.0 %collective-permute-start.3 = (f32[65,10,1]{0,1,2:T(8,128)S(1)}, f32[65,10,1]{0,1,2:T(8,128)S(1)}, u32[]{:S(2)}, u32[]{:S(2)}) collective-permute-start(f32[65,10,1]{0,1,2:T(8,128)S(1)} %copy.43), channel_id=1, source_target_pairs={{1,0},{2,1},{3,2},{4,3},{5,4},{6,5},{7,6},{9,8},{10,9},{11,10},{12... | collective-permute-start | bytes 7808 | tf_op jit(solution)/shard_map/ppermute | solution.py:18
  28.5 0.0 collective-permute-done.2
  28.5 0.3 copy.44
  28.8 1.6 collective-permute-done.3
  30.4 0.3 copy.45
  30.8 0.0 copy-done.2
  30.8 0.0 copy-start.6
  30.8 0.1 fusion.30
  30.9 0.1 fusion.34
  30.9 1.8 fusion.17
  32.7 0.0 all-gather.2.cloned.1.call-update
  32.7 0.0 reduce-scatter.2.cloned.1.call-start
  32.9 38.9 %all-gather.2.cloned.1.call-done = bf16[64,8,2048]{2,1,0:T(8,128)(2,1)} async-done(((bf16[64,8,256]{2,1,0:T(8,128)(2,1)}), bf16[64,8,2048]{2,1,0:T(8,128)(2,1)}) %all-gather.2.cloned.1.call-update) | async-done | bytes 2097168 | tf_op jit(solution)/shard_map/all_gather | solution.py:54
  71.7 2.9 reshape.238
  74.6 2.7 copy.50
  77.3 2.3 gather_fusion
  79.6 0.9 multiply_reduce_fusion
  80.5 0.1 select_bitcast_fusion.1
  80.6 0.8 select_bitcast_fusion
  81.4 2.5 broadcast_in_dim.67
  83.9 9.0 %scatter_fusion = f32[64,128,128]{2,0,1:T(8,128)} fusion(f32[64,128,128]{2,0,1:T(8,128)} %broadcast_in_dim.67, s32[64]{0:T(128)S(1)} %fusion.36, f32[64,64,128]{2,1,0:T(8,128)S(1)} %select_bitcast_fusion), kind=kCustom, calls=%fused_computation.1 | custom fusion | flops 524288 | bytes 6291712 | tf_op jit(solution)/shard_map/scatter-add | solution.py:71
  92.9 0.0 reduce-scatter.2.cloned.1.call-update
  92.9 44.1 %reduce-scatter.2.cloned.1.call-done = f32[2,64,8,128]{3,1,2,0:T(8,128)} async-done(((f32[16,64,8,128]{3,1,2,0:T(8,128)}), f32[2,64,8,128]{3,1,2,0:T(8,128)}) %reduce-scatter.2.cloned.1.call-update) | async-done | bytes 524304 | tf_op jit(solution)/shard_map/reduce_scatter | solution.py:73
  137.0 1.3 copy.63
  138.3 0.0 copy-start
  138.4 0.0 copy-start.3
  138.4 0.1 fusion.41
  138.5 1.3 collective-permute-start.4
  139.8 4.0 %collective-permute-start.5 = (f32[64,1,256]{2,1,0:T(1,128)S(1)}, f32[64,1,256]{2,1,0:T(1,128)S(1)}, u32[]{:S(2)}, u32[]{:S(2)}) collective-permute-start(f32[64,1,256]{2,1,0:T(1,128)S(1)} %get-tuple-element.13), channel_id=1, source_target_pairs={{0,8},{8,16},{16,24},{24,32},{32,40},{40,48},{48,56},{56,64},{64,7... | collective-permute-start | bytes 196616 | tf_op jit(solution)/shard_map/ppermute | solution.py:15
  144.4 0.0 collective-permute-done.4
  144.4 0.7 collective-permute-done.5
  145.1 0.2 pad_maximum_fusion.1
  145.3 0.2 fusion.40
  145.5 6.2 %collective-permute-start.6 = (f32[64,10,1]{2,1,0:T(8,128)S(1)}, f32[64,10,1]{2,1,0:T(8,128)S(1)}, u32[]{:S(2)}, u32[]{:S(2)}) collective-permute-start(f32[64,10,1]{2,1,0:T(8,128)S(1)} %get-tuple-element.9), channel_id=1, source_target_pairs={{1,0},{2,1},{3,2},{4,3},{5,4},{6,5},{7,6},{9,8},{10,9},{11,10},{12... | collective-permute-start | bytes 7688 | tf_op jit(solution)/shard_map/ppermute | solution.py:18
  151.6 1.9 collective-permute-start.7
  153.6 2.5 collective-permute-done.6
  156.1 3.6 %collective-permute-done.7 = f32[64,10,1]{2,1,0:T(8,128)S(1)} collective-permute-done((f32[64,10,1]{2,1,0:T(8,128)S(1)}, f32[64,10,1]{2,1,0:T(8,128)S(1)}, u32[]{:S(2)}, u32[]{:S(2)}) %collective-permute-start.7) | collective-permute-done | bytes 2592 | tf_op jit(solution)/shard_map/ppermute | solution.py:15
  159.7 0.8 convert_add_fusion
  160.5 0.7 fusion
  161.2 106.3 %psum.7 = f32[64,64]{0,1:T(8,128)S(1)} all-reduce(f32[64,64]{0,1:T(8,128)S(1)} %fusion), channel_id=1, replica_groups=mesh['mesh'=64,'obs'=8] {'mesh','obs'}, use_global_device_ids=true, to_apply=%region_3.4 | all-reduce | flops 4096 | bytes 32768 | tf_op jit(solution)/shard_map/psum | solution.py:89
  267.6 0.1 copy.55
  267.7 5.8 %cholesky.15 = f32[64,64]{1,0:T(8,128)S(1)} custom-call(f32[64,64]{1,0:T(8,128)S(1)} %fusion.29), custom_call_target="Cholesky" | custom-call | tf_op jit(solution)/shard_map/jit(cholesky)/cholesky | solution.py:89
  273.5 0.6 compare_reduce_fusion
  274.2 1.3 select_bitcast_fusion.2
  275.4 4.9 %custom-call.6 = f32[1,64,64]{1,2,0:T(8,128)S(1)} custom-call(f32[1,64,64]{2,1,0:T(8,128)S(1)} %get-tuple-element.2), custom_call_target="InvertDiagBlocksLowerTriangular" | custom-call | tf_op jit(solution)/shard_map/triangular_solve | solution.py:90
  280.3 0.2 copy.58
  280.5 0.6 convolution_select_fusion
  281.2 1.0 copy.59
  (17 shorter events, 0.1 us)
Async XLA Ops:
  7.2 64.5 %all-gather.2.cloned.1.call-start = ((), (), s32[]{:S(2)}) async-start(), calls=%async_computation.1 | async-start | bytes 2359296 | tf_op jit(solution)/shard_map/all_gather | solution.py:54
  9.1 5.8 %collective-permute-start = (f32[65,1,256]{2,0,1:T(8,128)S(1)}, f32[65,1,256]{2,0,1:T(8,128)S(1)}, u32[]{:S(2)}, u32[]{:S(2)}) collective-permute-start(f32[65,1,256]{2,0,1:T(8,128)S(1)} %copy.38), channel_id=1, source_target_pairs={{0,8},{8,16},{16,24},{24,32},{32,40},{40,48},{48,56},{56,64},{64,7... | collective-permute-start | bytes 199688 | tf_op jit(solution)/shard_map/ppermute | solution.py:15
  13.5 5.3 %collective-permute-start.1 = (f32[65,1,256]{2,0,1:T(8,128)S(1)}, f32[65,1,256]{2,0,1:T(8,128)S(1)}, u32[]{:S(2)}, u32[]{:S(2)}) collective-permute-start(f32[65,1,256]{2,0,1:T(8,128)S(1)} %copy.39), channel_id=1, source_target_pairs={{8,0},{16,8},{24,16},{32,24},{40,32},{48,40},{56,48},{64,56},{72,6... | collective-permute-start | bytes 199688 | tf_op jit(solution)/shard_map/ppermute | solution.py:18
  19.7 11.0 %copy-start.2 = (f32[8,256]{1,0:T(8,128)S(1)}, f32[8,256]{1,0:T(8,128)}, u32[]{:S(2)}) copy-start(f32[8,256]{1,0:T(8,128)} %param.10) | copy-start | bytes 24580
  19.9 11.0 %copy-start.4 = (f32[8,256]{1,0:T(8,128)S(1)}, f32[8,256]{1,0:T(8,128)}, u32[]{:S(2)}) copy-start(f32[8,256]{1,0:T(8,128)} %param.11) | copy-start | bytes 24580
  20.2 8.2 %collective-permute-start.2 = (f32[65,10,1]{0,1,2:T(8,128)S(1)}, f32[65,10,1]{0,1,2:T(8,128)S(1)}, u32[]{:S(2)}, u32[]{:S(2)}) collective-permute-start(f32[65,10,1]{0,1,2:T(8,128)S(1)} %copy.42), channel_id=1, source_target_pairs={{0,1},{1,2},{2,3},{3,4},{4,5},{5,6},{6,7},{8,9},{9,10},{10,11},{11... | collective-permute-start | bytes 7808 | tf_op jit(solution)/shard_map/ppermute | solution.py:15
  25.4 5.0 %collective-permute-start.3 = (f32[65,10,1]{0,1,2:T(8,128)S(1)}, f32[65,10,1]{0,1,2:T(8,128)S(1)}, u32[]{:S(2)}, u32[]{:S(2)}) collective-permute-start(f32[65,10,1]{0,1,2:T(8,128)S(1)} %copy.43), channel_id=1, source_target_pairs={{1,0},{2,1},{3,2},{4,3},{5,4},{6,5},{7,6},{9,8},{10,9},{11,10},{12... | collective-permute-start | bytes 7808 | tf_op jit(solution)/shard_map/ppermute | solution.py:18
  30.8 2.0 copy-start.6
  32.7 104.3 %reduce-scatter.2.cloned.1.call-start = ((), (), s32[]{:S(2)}) async-start(), calls=%async_computation.2 | async-start | bytes 4718592 | tf_op jit(solution)/shard_map/reduce_scatter | solution.py:73
  77.3 2.4 copy-start.1
  77.3 3.2 %copy-start.5 = (f32[1,64]{1,0:T(1,128)S(1)}, f32[1,64]{1,0:T(1,128)}, u32[]{:S(2)}) copy-start(f32[1,64]{1,0:T(1,128)} %param.14) | copy-start | bytes 772
  138.3 21.3 %copy-start = (bf16[64,8,256]{2,1,0:T(8,128)(2,1)S(1)}, bf16[64,8,256]{2,1,0:T(8,128)(2,1)}, u32[]{:S(2)}) copy-start(bf16[64,8,256]{2,1,0:T(8,128)(2,1)} %param.8) | copy-start | bytes 786436
  138.4 21.3 %copy-start.3 = (f32[8,256]{1,0:T(8,128)S(1)}, f32[8,256]{1,0:T(8,128)}, u32[]{:S(2)}) copy-start(f32[8,256]{1,0:T(8,128)} %param.9) | copy-start | bytes 24580
  138.5 5.9 %collective-permute-start.4 = (f32[64,1,256]{2,1,0:T(1,128)S(1)}, f32[64,1,256]{2,1,0:T(1,128)S(1)}, u32[]{:S(2)}, u32[]{:S(2)}) collective-permute-start(f32[64,1,256]{2,1,0:T(1,128)S(1)} %get-tuple-element.14), channel_id=1, source_target_pairs={{8,0},{16,8},{24,16},{32,24},{40,32},{48,40},{56,48},{64,56},{72,6... | collective-permute-start | bytes 196616 | tf_op jit(solution)/shard_map/ppermute | solution.py:18
  139.8 5.3 %collective-permute-start.5 = (f32[64,1,256]{2,1,0:T(1,128)S(1)}, f32[64,1,256]{2,1,0:T(1,128)S(1)}, u32[]{:S(2)}, u32[]{:S(2)}) collective-permute-start(f32[64,1,256]{2,1,0:T(1,128)S(1)} %get-tuple-element.13), channel_id=1, source_target_pairs={{0,8},{8,16},{16,24},{24,32},{32,40},{40,48},{48,56},{56,64},{64,7... | collective-permute-start | bytes 196616 | tf_op jit(solution)/shard_map/ppermute | solution.py:15
  145.5 10.6 %collective-permute-start.6 = (f32[64,10,1]{2,1,0:T(8,128)S(1)}, f32[64,10,1]{2,1,0:T(8,128)S(1)}, u32[]{:S(2)}, u32[]{:S(2)}) collective-permute-start(f32[64,10,1]{2,1,0:T(8,128)S(1)} %get-tuple-element.9), channel_id=1, source_target_pairs={{1,0},{2,1},{3,2},{4,3},{5,4},{6,5},{7,6},{9,8},{10,9},{11,10},{12... | collective-permute-start | bytes 7688 | tf_op jit(solution)/shard_map/ppermute | solution.py:18
  151.6 8.0 %collective-permute-start.7 = (f32[64,10,1]{2,1,0:T(8,128)S(1)}, f32[64,10,1]{2,1,0:T(8,128)S(1)}, u32[]{:S(2)}, u32[]{:S(2)}) collective-permute-start(f32[64,10,1]{2,1,0:T(8,128)S(1)} %get-tuple-element.10), channel_id=1, source_target_pairs={{0,1},{1,2},{2,3},{3,4},{4,5},{5,6},{6,7},{8,9},{9,10},{10,11},{11... | collective-permute-start | bytes 7688 | tf_op jit(solution)/shard_map/ppermute | solution.py:15
Sparse Core Ops, SparseCore 0:
  32.8 38.8 all-gather.1
  93.0 43.9 reduce-scatter.1
where the time goes:
time: 290 us; the launch traced here: 289 us
  blocking collectives  106 us (37%)
  waiting for transfers between devices  95.2 us (33%)
  other arithmetic  29.1 us (10%)
  starting transfers between devices  27 us (9%)
  between operations  15 us (5%)
  local copies, waits for them, and re-layouts  14.9 us (5%)
    psum x1, blocking collectives, per_device(): factor = jnp.linalg.cholesky(lax.psum(local_gram, ('mesh', 'obs')))  106 us
    reduce_scatter x1, waiting for transfers between devices, per_device(): lax.psum_scatter(partial_value.reshape(probe_count, amount, rows_here, BL...  44.1 us
    all_gather x1, waiting for transfers between devices, per_device(): segment = lax.all_gather(tangent, 'obs', axis=2, tiled=True)  38.9 us
    ppermute x4, starting transfers between devices, extended(): lax.ppermute(lax.slice_in_dim(block, block.shape[dim] - width, None, axis...  15.2 us
    ppermute x4, starting transfers between devices, extended(): lax.ppermute(lax.slice_in_dim(block, 0, width, axis=dim), axis, backward)  11.8 us
    scatter-add x1, other arithmetic, per_device(): partial_value = jnp.zeros((probe_count, amount * rows_here, BLOCK), jnp.f...  9.02 us
    ppermute x4, waiting for transfers between devices, extended(): lax.ppermute(lax.slice_in_dim(block, 0, width, axis=dim), axis, backward)  7.92 us
    another operation x3, other arithmetic, per_device(): factor = jnp.linalg.cholesky(lax.psum(local_gram, ('mesh', 'obs')))  6.52 us
  transfers between devices with their start and end apart: 10, of which 8 were waited for; matrix products, arithmetic and copies ran while one was open for 0% of the time, Pallas kernels for 0%

commit v1 on v0

--- a/solution.py
+++ b/solution.py
@@ -5,6 +5,24 @@
 
 BLOCK = 128
 PRIOR = 1.0
+
+
+def gather_around(array, axis, dim):
+    ways, here, turn = (lax.axis_size(axis), lax.axis_index(axis), array.shape[dim])
+    shape = [n * ways if d == dim else n for d, n in enumerate(array.shape)]
+    full = lax.dynamic_update_slice_in_dim(
+        jnp.zeros(shape, array.dtype), array, here * turn, axis=dim
+    )
+    going_up = going_down = array
+    for far in range(1, ways // 2 + 1):
+        going_up = lax.ppermute(going_up, axis, [(d, (d + 1) % ways) for d in range(ways)])
+        full = lax.dynamic_update_slice_in_dim(full, going_up, (here - far) % ways * turn, axis=dim)
+        if 2 * far < ways:
+            going_down = lax.ppermute(going_down, axis, [(d, (d - 1) % ways) for d in range(ways)])
+            full = lax.dynamic_update_slice_in_dim(
+                full, going_down, (here + far) % ways * turn, axis=dim
+            )
+    return full
 
 
 def extended(block, sides, width):
@@ -51,7 +69,7 @@
     col_ids = obs_block[0] % slab_columns
     weights = obs_weight[0]
     precision = obs_prec[0]
-    segment = lax.all_gather(tangent, "obs", axis=2, tiled=True)
+    segment = gather_around(tangent, "obs", 2)
     seg_blocks = segment.shape[2] // BLOCK
     local_col = col_ids
     inside = (local_col >= 0) & (local_col < seg_blocks)

time: 290 us -> 277 us (0.955)
  waiting for transfers between devices: 95.2 us -> 73.1 us
  starting transfers between devices: 27 us -> 36.7 us
    all_gather x1 -> x0, waiting for transfers between devices: 38.9 us -> none  [per_device(): segment = lax.all_gather(tangent, 'obs', axis=2, tiled=True)]
    ppermute x0 -> x7, waiting for transfers between devices: none -> 11.3 us  [the longest x4 10.5 us: gather_around(): lax.ppermute(going_up, axis, [(d, (d + 1) % ways) for d in range(ways)])]
    ppermute x0 -> x7, starting transfers between devices: none -> 9.73 us  [the longest x4 7.49 us: gather_around(): lax.ppermute(going_up, axis, [(d, (d + 1) % ways) for d in range(ways)])]
    reduce_scatter x1, waiting for transfers between devices: 44.1 us -> 49.6 us  [per_device(): lax.psum_scatter(partial_value.reshape(probe_count, amount, rows_here, BL...]
  transfers between devices with their start and end apart: 10 -> 16, of which waited for: 8 -> 13; matrix products, arithmetic and copies ran while one was open for 0% -> 0% of each run, Pallas kernels for 0% -> 0%
where the time goes in v1:
time: 277 us; the launch traced here: 276 us
  blocking collectives  106 us (38%)
  waiting for transfers between devices  73.1 us (26%)
  starting transfers between devices  36.7 us (13%)
  other arithmetic  28.5 us (10%)
  between operations  15.1 us (5%)
  local copies, waits for them, and re-layouts  14.9 us (5%)
    psum x1, blocking collectives, per_device(): factor = jnp.linalg.cholesky(lax.psum(local_gram, ('mesh', 'obs')))  106 us
    reduce_scatter x1, waiting for transfers between devices, per_device(): lax.psum_scatter(partial_value.reshape(probe_count, amount, rows_here, BL...  49.6 us
    ppermute x4, starting transfers between devices, extended(): lax.ppermute(lax.slice_in_dim(block, block.shape[dim] - width, None, axis...  15.2 us
    ppermute x4, starting transfers between devices, extended(): lax.ppermute(lax.slice_in_dim(block, 0, width, axis=dim), axis, backward)  11.7 us
    ppermute x4, waiting for transfers between devices, gather_around(): lax.ppermute(going_up, axis, [(d, (d + 1) % ways) for d in range(ways)])  10.5 us
    scatter-add x1, other arithmetic, per_device(): partial_value = jnp.zeros((probe_count, amount * rows_here, BLOCK), jnp.f...  9.07 us
    ppermute x4, waiting for transfers between devices, extended(): lax.ppermute(lax.slice_in_dim(block, 0, width, axis=dim), axis, backward)  7.94 us
    ppermute x4, starting transfers between devices, gather_around(): lax.ppermute(going_up, axis, [(d, (d + 1) % ways) for d in range(ways)])  7.49 us
  transfers between devices with their start and end apart: 16, of which 13 were waited for; matrix products, arithmetic and copies ran while one was open for 0% of the time, Pallas kernels for 0%

profile of v1, /device:TPU:1, one launch (start us, length us, event | category | flops | bytes accessed | tf_op | source)
XLA Modules:
  0.0 276.0 jit_solution(1124678791842772861)
XLA Ops:
  7.2 1.0 convert_multiply_fusion
  8.2 0.9 pad_maximum_fusion.23
  9.1 4.4 %collective-permute-start = (f32[65,1,256]{2,0,1:T(8,128)S(1)}, f32[65,1,256]{2,0,1:T(8,128)S(1)}, u32[]{:S(2)}, u32[]{:S(2)}) collective-permute-start(f32[65,1,256]{2,0,1:T(8,128)S(1)} %copy.45), channel_id=1, source_target_pairs={{0,8},{8,16},{16,24},{24,32},{32,40},{40,48},{48,56},{56,64},{64,7... | collective-permute-start | bytes 199688 | tf_op jit(solution)/shard_map/ppermute | solution.py:33
  13.5 1.3 collective-permute-start.1
  14.8 0.1 collective-permute-done
  14.9 3.8 %collective-permute-done.1 = f32[65,1,256]{2,0,1:T(8,128)S(1)} collective-permute-done((f32[65,1,256]{2,0,1:T(8,128)S(1)}, f32[65,1,256]{2,0,1:T(8,128)S(1)}, u32[]{:S(2)}, u32[]{:S(2)}) %collective-permute-start.1) | collective-permute-done | bytes 66592 | tf_op jit(solution)/shard_map/ppermute | solution.py:36
  18.8 0.9 pad_maximum_fusion
  19.8 0.2 fusion.40
  20.0 0.3 copy.49
  20.2 4.9 %collective-permute-start.2 = (f32[65,10,1]{0,1,2:T(8,128)S(1)}, f32[65,10,1]{0,1,2:T(8,128)S(1)}, u32[]{:S(2)}, u32[]{:S(2)}) collective-permute-start(f32[65,10,1]{0,1,2:T(8,128)S(1)} %copy.49), channel_id=1, source_target_pairs={{0,1},{1,2},{2,3},{3,4},{4,5},{5,6},{6,7},{8,9},{9,10},{10,11},{11... | collective-permute-start | bytes 7808 | tf_op jit(solution)/shard_map/ppermute | solution.py:33
  25.2 0.3 copy.50
  25.4 3.0 %collective-permute-start.3 = (f32[65,10,1]{0,1,2:T(8,128)S(1)}, f32[65,10,1]{0,1,2:T(8,128)S(1)}, u32[]{:S(2)}, u32[]{:S(2)}) collective-permute-start(f32[65,10,1]{0,1,2:T(8,128)S(1)} %copy.50), channel_id=1, source_target_pairs={{1,0},{2,1},{3,2},{4,3},{5,4},{6,5},{7,6},{9,8},{10,9},{11,10},{12... | collective-permute-start | bytes 7808 | tf_op jit(solution)/shard_map/ppermute | solution.py:36
  28.5 0.3 copy.51
  28.8 1.6 collective-permute-done.3
  30.4 0.3 copy.52
  30.8 0.1 fusion.30
  30.9 0.1 fusion.34
  30.9 0.6 copy-done
  31.6 0.2 broadcast_in_dim.74
  31.8 0.8 copy-done.1
  32.6 1.1 constant_dynamic-update-slice_fusion.7
  33.8 0.5 collective-permute-start.5
  34.3 2.8 %collective-permute-done.4 = bf16[64,8,256]{2,1,0:T(8,128)(2,1)S(1)} collective-permute-done((bf16[64,8,256]{2,1,0:T(8,128)(2,1)S(1)}, bf16[64,8,256]{2,1,0:T(8,128)(2,1)S(1)}, u32[]{:S(2)}, u32[]{:S(2)}) %collective-permute-start.4) | collective-permute-done | bytes 262176 | tf_op jit(solution)/shard_map/ppermute | solution.py:18
  37.1 2.5 collective-permute-start.6
  39.6 0.4 collective-permute-start.7
  40.0 2.9 %collective-permute-done.6 = bf16[64,8,256]{2,1,0:T(8,128)(2,1)S(1)} collective-permute-done((bf16[64,8,256]{2,1,0:T(8,128)(2,1)S(1)}, bf16[64,8,256]{2,1,0:T(8,128)(2,1)S(1)}, u32[]{:S(2)}, u32[]{:S(2)}) %collective-permute-start.6) | collective-permute-done | bytes 262176 | tf_op jit(solution)/shard_map/ppermute | solution.py:18
  42.9 2.5 collective-permute-start.8
  45.4 0.3 collective-permute-done.7
  45.7 1.4 collective-permute-start.9
  47.1 1.6 collective-permute-done.8
  48.7 2.5 collective-permute-start.10
  51.2 0.6 collective-permute-done.9
  51.8 3.2 %collective-permute-done.10 = bf16[64,8,256]{2,1,0:T(8,128)(2,1)S(1)} collective-permute-done((bf16[64,8,256]{2,1,0:T(8,128)(2,1)S(1)}, bf16[64,8,256]{2,1,0:T(8,128)(2,1)S(1)}, u32[]{:S(2)}, u32[]{:S(2)}) %collective-permute-start.10) | collective-permute-done | bytes 262176 | tf_op jit(solution)/shard_map/ppermute | solution.py:18
  55.0 2.4 reshape.238
  57.4 2.9 %copy.57 = bf16[64,128,128]{2,0,1:T(8,128)(2,1)S(1)} copy(bf16[64,128,128]{2,1,0:T(8,128)(2,1)} %reshape.238) | data formatting | bytes 4194304 | tf_op jit(solution)/shard_map/reshape | solution.py:77
  60.4 0.7 gather_fusion
  61.1 0.9 multiply_reduce_fusion
  62.0 0.1 select_bitcast_fusion.1
  62.1 0.8 select_bitcast_fusion
  62.9 2.5 broadcast_in_dim.70
  65.3 9.1 %scatter_fusion = f32[64,128,128]{2,0,1:T(8,128)} fusion(f32[64,128,128]{2,0,1:T(8,128)} %broadcast_in_dim.70, s32[64]{0:T(128)S(1)} %fusion.36, f32[64,64,128]{2,1,0:T(8,128)S(1)} %select_bitcast_fusion), kind=kCustom, calls=%fused_computation.1 | custom fusion | flops 524288 | bytes 6291712 | tf_op jit(solution)/shard_map/scatter-add | solution.py:89
  74.4 49.6 %reduce-scatter.2.cloned.1.call-done = f32[2,64,8,128]{3,1,2,0:T(8,128)} async-done(((f32[16,64,8,128]{3,1,2,0:T(8,128)}), f32[2,64,8,128]{3,1,2,0:T(8,128)}) %reduce-scatter.2.cloned.1.call-update) | async-done | bytes 524304 | tf_op jit(solution)/shard_map/reduce_scatter | solution.py:91
  124.0 1.3 copy.70
  125.4 0.1 fusion.42
  125.5 1.3 collective-permute-start.11
  126.8 4.0 %collective-permute-start.12 = (f32[64,1,256]{2,1,0:T(1,128)S(1)}, f32[64,1,256]{2,1,0:T(1,128)S(1)}, u32[]{:S(2)}, u32[]{:S(2)}) collective-permute-start(f32[64,1,256]{2,1,0:T(1,128)S(1)} %get-tuple-element.15), channel_id=1, source_target_pairs={{0,8},{8,16},{16,24},{24,32},{32,40},{40,48},{48,56},{56,64},{64,7... | collective-permute-start | bytes 196616 | tf_op jit(solution)/shard_map/ppermute | solution.py:33
  131.4 0.7 collective-permute-done.12
  132.1 0.2 pad_maximum_fusion.1
  132.3 0.2 fusion.41
  132.5 6.1 %collective-permute-start.13 = (f32[64,10,1]{2,1,0:T(8,128)S(1)}, f32[64,10,1]{2,1,0:T(8,128)S(1)}, u32[]{:S(2)}, u32[]{:S(2)}) collective-permute-start(f32[64,10,1]{2,1,0:T(8,128)S(1)} %get-tuple-element.11), channel_id=1, source_target_pairs={{1,0},{2,1},{3,2},{4,3},{5,4},{6,5},{7,6},{9,8},{10,9},{11,10},{12... | collective-permute-start | bytes 7688 | tf_op jit(solution)/shard_map/ppermute | solution.py:36
  138.6 1.9 collective-permute-start.14
  140.6 2.5 collective-permute-done.13
  143.1 3.6 %collective-permute-done.14 = f32[64,10,1]{2,1,0:T(8,128)S(1)} collective-permute-done((f32[64,10,1]{2,1,0:T(8,128)S(1)}, f32[64,10,1]{2,1,0:T(8,128)S(1)}, u32[]{:S(2)}, u32[]{:S(2)}) %collective-permute-start.14) | collective-permute-done | bytes 2592 | tf_op jit(solution)/shard_map/ppermute | solution.py:33
  146.6 0.8 convert_add_fusion
  147.5 0.7 fusion
  148.2 106.4 %psum.7 = f32[64,64]{0,1:T(8,128)S(1)} all-reduce(f32[64,64]{0,1:T(8,128)S(1)} %fusion), channel_id=1, replica_groups=mesh['mesh'=64,'obs'=8] {'mesh','obs'}, use_global_device_ids=true, to_apply=%region_3.4 | all-reduce | flops 4096 | bytes 32768 | tf_op jit(solution)/shard_map/psum | solution.py:107
  254.6 0.1 copy.62
  254.7 5.8 %cholesky.15 = f32[64,64]{1,0:T(8,128)S(1)} custom-call(f32[64,64]{1,0:T(8,128)S(1)} %fusion.29), custom_call_target="Cholesky" | custom-call | tf_op jit(solution)/shard_map/jit(cholesky)/cholesky | solution.py:107
  260.6 0.6 compare_reduce_fusion
  261.2 1.3 select_bitcast_fusion.2
  262.5 4.9 %custom-call.6 = f32[1,64,64]{1,2,0:T(8,128)S(1)} custom-call(f32[1,64,64]{2,1,0:T(8,128)S(1)} %get-tuple-element.2), custom_call_target="InvertDiagBlocksLowerTriangular" | custom-call | tf_op jit(solution)/shard_map/triangular_solve | solution.py:108
  267.4 0.2 copy.65
  267.6 0.6 convolution_select_fusion
  268.2 1.0 copy.66
  (40 shorter events, 0.6 us)
Async XLA Ops:
  7.2 116.8 %reduce-scatter.2.cloned.1.call-start = ((), (), s32[]{:S(2)}) async-start(), calls=%async_computation.1 | async-start | bytes 4718592 | tf_op jit(solution)/shard_map/reduce_scatter | solution.py:91
  9.1 5.8 %collective-permute-start = (f32[65,1,256]{2,0,1:T(8,128)S(1)}, f32[65,1,256]{2,0,1:T(8,128)S(1)}, u32[]{:S(2)}, u32[]{:S(2)}) collective-permute-start(f32[65,1,256]{2,0,1:T(8,128)S(1)} %copy.45), channel_id=1, source_target_pairs={{0,8},{8,16},{16,24},{24,32},{32,40},{40,48},{48,56},{56,64},{64,7... | collective-permute-start | bytes 199688 | tf_op jit(solution)/shard_map/ppermute | solution.py:33
  13.5 5.3 %collective-permute-start.1 = (f32[65,1,256]{2,0,1:T(8,128)S(1)}, f32[65,1,256]{2,0,1:T(8,128)S(1)}, u32[]{:S(2)}, u32[]{:S(2)}) collective-permute-start(f32[65,1,256]{2,0,1:T(8,128)S(1)} %copy.46), channel_id=1, source_target_pairs={{8,0},{16,8},{24,16},{32,24},{40,32},{48,40},{56,48},{64,56},{72,6... | collective-permute-start | bytes 199688 | tf_op jit(solution)/shard_map/ppermute | solution.py:36
  19.7 11.0 %copy-start.4 = (f32[8,256]{1,0:T(8,128)S(1)}, f32[8,256]{1,0:T(8,128)}, u32[]{:S(2)}) copy-start(f32[8,256]{1,0:T(8,128)} %param.10) | copy-start | bytes 24580
  20.2 8.2 %collective-permute-start.2 = (f32[65,10,1]{0,1,2:T(8,128)S(1)}, f32[65,10,1]{0,1,2:T(8,128)S(1)}, u32[]{:S(2)}, u32[]{:S(2)}) collective-permute-start(f32[65,10,1]{0,1,2:T(8,128)S(1)} %copy.49), channel_id=1, source_target_pairs={{0,1},{1,2},{2,3},{3,4},{4,5},{5,6},{6,7},{8,9},{9,10},{10,11},{11... | collective-permute-start | bytes 7808 | tf_op jit(solution)/shard_map/ppermute | solution.py:33
  25.4 5.0 %collective-permute-start.3 = (f32[65,10,1]{0,1,2:T(8,128)S(1)}, f32[65,10,1]{0,1,2:T(8,128)S(1)}, u32[]{:S(2)}, u32[]{:S(2)}) collective-permute-start(f32[65,10,1]{0,1,2:T(8,128)S(1)} %copy.50), channel_id=1, source_target_pairs={{1,0},{2,1},{3,2},{4,3},{5,4},{6,5},{7,6},{9,8},{10,9},{11,10},{12... | collective-permute-start | bytes 7808 | tf_op jit(solution)/shard_map/ppermute | solution.py:36
  30.8 0.8 copy-start
  30.8 1.1 copy-start.6
  31.6 1.0 copy-start.1
  31.6 2.2 copy-start.8
  33.7 3.4 %collective-permute-start.4 = (bf16[64,8,256]{2,1,0:T(8,128)(2,1)S(1)}, bf16[64,8,256]{2,1,0:T(8,128)(2,1)S(1)}, u32[]{:S(2)}, u32[]{:S(2)}) collective-permute-start(bf16[64,8,256]{2,1,0:T(8,128)(2,1)S(1)} %get-tuple-element.8), channel_id=1, source_target_pairs={{0,1},{1,2},{2,3},{3,4},{4,5},{5,6},{6,7},{7,0},{8,9},{9,10},{10,1... | collective-permute-start | bytes 786440 | tf_op jit(solution)/shard_map/ppermute | solution.py:18
  33.8 5.8 %collective-permute-start.5 = (bf16[64,8,256]{2,1,0:T(8,128)(2,1)S(1)}, bf16[64,8,256]{2,1,0:T(8,128)(2,1)S(1)}, u32[]{:S(2)}, u32[]{:S(2)}) collective-permute-start(bf16[64,8,256]{2,1,0:T(8,128)(2,1)S(1)} %get-tuple-element.8), channel_id=1, source_target_pairs={{0,7},{1,0},{2,1},{3,2},{4,3},{5,4},{6,5},{7,6},{8,15},{9,8},{10,9... | collective-permute-start | bytes 786440 | tf_op jit(solution)/shard_map/ppermute | solution.py:21
  37.1 5.8 %collective-permute-start.6 = (bf16[64,8,256]{2,1,0:T(8,128)(2,1)S(1)}, bf16[64,8,256]{2,1,0:T(8,128)(2,1)S(1)}, u32[]{:S(2)}, u32[]{:S(2)}) collective-permute-start(bf16[64,8,256]{2,1,0:T(8,128)(2,1)S(1)} %collective-permute-done.4), channel_id=1, source_target_pairs={{0,1},{1,2},{2,3},{3,4},{4,5},{5,6},{6,7},{7,0},{8,9},{9,10},{10,1... | collective-permute-start | bytes 786440 | tf_op jit(solution)/shard_map/ppermute | solution.py:18
  39.6 6.1 %collective-permute-start.7 = (bf16[64,8,256]{2,1,0:T(8,128)(2,1)S(1)}, bf16[64,8,256]{2,1,0:T(8,128)(2,1)S(1)}, u32[]{:S(2)}, u32[]{:S(2)}) collective-permute-start(bf16[64,8,256]{2,1,0:T(8,128)(2,1)S(1)} %collective-permute-done.5), channel_id=1, source_target_pairs={{0,7},{1,0},{2,1},{3,2},{4,3},{5,4},{6,5},{7,6},{8,15},{9,8},{10,9... | collective-permute-start | bytes 786440 | tf_op jit(solution)/shard_map/ppermute | solution.py:21
  42.9 5.8 %collective-permute-start.8 = (bf16[64,8,256]{2,1,0:T(8,128)(2,1)S(1)}, bf16[64,8,256]{2,1,0:T(8,128)(2,1)S(1)}, u32[]{:S(2)}, u32[]{:S(2)}) collective-permute-start(bf16[64,8,256]{2,1,0:T(8,128)(2,1)S(1)} %collective-permute-done.6), channel_id=1, source_target_pairs={{0,1},{1,2},{2,3},{3,4},{4,5},{5,6},{6,7},{7,0},{8,9},{9,10},{10,1... | collective-permute-start | bytes 786440 | tf_op jit(solution)/shard_map/ppermute | solution.py:18
  45.7 6.1 %collective-permute-start.9 = (bf16[64,8,256]{2,1,0:T(8,128)(2,1)S(1)}, bf16[64,8,256]{2,1,0:T(8,128)(2,1)S(1)}, u32[]{:S(2)}, u32[]{:S(2)}) collective-permute-start(bf16[64,8,256]{2,1,0:T(8,128)(2,1)S(1)} %collective-permute-done.7), channel_id=1, source_target_pairs={{0,7},{1,0},{2,1},{3,2},{4,3},{5,4},{6,5},{7,6},{8,15},{9,8},{10,9... | collective-permute-start | bytes 786440 | tf_op jit(solution)/shard_map/ppermute | solution.py:21
  48.7 6.3 %collective-permute-start.10 = (bf16[64,8,256]{2,1,0:T(8,128)(2,1)S(1)}, bf16[64,8,256]{2,1,0:T(8,128)(2,1)S(1)}, u32[]{:S(2)}, u32[]{:S(2)}) collective-permute-start(bf16[64,8,256]{2,1,0:T(8,128)(2,1)S(1)} %collective-permute-done.8), channel_id=1, source_target_pairs={{0,1},{1,2},{2,3},{3,4},{4,5},{5,6},{6,7},{7,0},{8,9},{9,10},{10,1... | collective-permute-start | bytes 786440 | tf_op jit(solution)/shard_map/ppermute | solution.py:18
  60.3 0.8 copy-start.3
  60.3 1.7 copy-start.7
  125.3 21.3 %copy-start.2 = (bf16[64,8,256]{2,1,0:T(8,128)(2,1)S(1)}, bf16[64,8,256]{2,1,0:T(8,128)(2,1)}, u32[]{:S(2)}) copy-start(bf16[64,8,256]{2,1,0:T(8,128)(2,1)} %param.8) | copy-start | bytes 786436
  125.4 21.3 %copy-start.5 = (f32[8,256]{1,0:T(8,128)S(1)}, f32[8,256]{1,0:T(8,128)}, u32[]{:S(2)}) copy-start(f32[8,256]{1,0:T(8,128)} %param.9) | copy-start | bytes 24580
  125.5 5.9 %collective-permute-start.11 = (f32[64,1,256]{2,1,0:T(1,128)S(1)}, f32[64,1,256]{2,1,0:T(1,128)S(1)}, u32[]{:S(2)}, u32[]{:S(2)}) collective-permute-start(f32[64,1,256]{2,1,0:T(1,128)S(1)} %get-tuple-element.16), channel_id=1, source_target_pairs={{8,0},{16,8},{24,16},{32,24},{40,32},{48,40},{56,48},{64,56},{72,6... | collective-permute-start | bytes 196616 | tf_op jit(solution)/shard_map/ppermute | solution.py:36
  126.8 5.3 %collective-permute-start.12 = (f32[64,1,256]{2,1,0:T(1,128)S(1)}, f32[64,1,256]{2,1,0:T(1,128)S(1)}, u32[]{:S(2)}, u32[]{:S(2)}) collective-permute-start(f32[64,1,256]{2,1,0:T(1,128)S(1)} %get-tuple-element.15), channel_id=1, source_target_pairs={{0,8},{8,16},{16,24},{24,32},{32,40},{40,48},{48,56},{56,64},{64,7... | collective-permute-start | bytes 196616 | tf_op jit(solution)/shard_map/ppermute | solution.py:33
  132.5 10.6 %collective-permute-start.13 = (f32[64,10,1]{2,1,0:T(8,128)S(1)}, f32[64,10,1]{2,1,0:T(8,128)S(1)}, u32[]{:S(2)}, u32[]{:S(2)}) collective-permute-start(f32[64,10,1]{2,1,0:T(8,128)S(1)} %get-tuple-element.11), channel_id=1, source_target_pairs={{1,0},{2,1},{3,2},{4,3},{5,4},{6,5},{7,6},{9,8},{10,9},{11,10},{12... | collective-permute-start | bytes 7688 | tf_op jit(solution)/shard_map/ppermute | solution.py:36
  138.6 8.0 %collective-permute-start.14 = (f32[64,10,1]{2,1,0:T(8,128)S(1)}, f32[64,10,1]{2,1,0:T(8,128)S(1)}, u32[]{:S(2)}, u32[]{:S(2)}) collective-permute-start(f32[64,10,1]{2,1,0:T(8,128)S(1)} %get-tuple-element.12), channel_id=1, source_target_pairs={{0,1},{1,2},{2,3},{3,4},{4,5},{5,6},{6,7},{8,9},{9,10},{10,11},{11... | collective-permute-start | bytes 7688 | tf_op jit(solution)/shard_map/ppermute | solution.py:33
Sparse Core Ops, SparseCore 0:
  74.6 49.3 reduce-scatter.1
